TPU v7x, 512 devices: a whole 4x4x16 slice. The times are simulated.
512 devices in a mesh: row: 16 (over y, x), col: 32 (over z, core).
Axes of the slice: x: 4, y: 4, z: 16, core: 2. Of those that a mesh axis runs over, the one named last changes fastest.
Arguments:
- panel: bfloat16 [4, 16, 512, 512], P(None, 'row', 'col'), may hold values from -1.1953125 to 1.1953125
- inverse_factor: bfloat16 [512, 512], replicated
- slot_rows: int32 [16, 32, 2], P('row', 'col'), may hold values from 0 to 63, as said below
- slot_cols: int32 [16, 32, 2], P('row', 'col'), may hold values from 0 to 63, as said below
- live_count: int32 [16, 32], P('row', 'col'), may hold values from 0 to 2
Outputs:
- contrib: bfloat16 [16, 32, 2, 512, 512], P('row', 'col')
Inputs may be any that keep to these rules, and one draw needn't show every extreme that they name: slot_rows[r, c, s] is congruent to r modulo 16; for s < live_count[r, c] the slots of one position name distinct blocks with slot_rows >= slot_cols; the other slots are ignored. slot_cols[r, c, s] is congruent to c modulo 32.
All inputs are finite; a program needn't handle non-finite values.
Results may differ from a plain program's by a relative error of at most 0.0054.
Values may be sent and summed in bfloat16 or wider, within the bound.
No kernel may reach another device: no remote copies, remote signals or barrier semaphores. Data moves between devices by JAX's collectives and lax.ppermute only.
A program may use at most 64 MiB of HBM per device.

v0:
```python
import jax
import jax.numpy as jnp
from jax import lax
from jax.sharding import PartitionSpec as P


def broadcast(value, axis, source):
    kept = jnp.where(lax.axis_index(axis) == source, value, 0).astype(value.dtype)
    return lax.psum(kept, axis)


def body(panel, inverse_factor, slot_rows, slot_cols, live_count):
    panel_count, _, part_rows, tile_width = panel.shape
    grid_rows = lax.axis_size("row")
    grid_cols = lax.axis_size("col")
    col_ratio = grid_cols // grid_rows
    column_count = panel_count // col_ratio
    solved = jnp.dot(
        panel.reshape(-1, tile_width), inverse_factor, preferred_element_type=jnp.float32
    )
    solved = solved.astype(jnp.bfloat16).reshape(panel_count, 1, part_rows, tile_width)
    row_blocks = lax.all_gather(solved, "col", axis=2, tiled=True).reshape(
        panel_count, tile_width, tile_width
    )
    position = lax.axis_index("col")
    grouped = row_blocks.reshape(column_count, col_ratio, tile_width, tile_width)
    picked = lax.dynamic_index_in_dim(grouped, position // grid_rows, 1, keepdims=False)
    col_blocks = broadcast(picked, "row", position % grid_rows)
    slot_total = slot_rows.shape[-1]
    rows_here = slot_rows.reshape(-1)
    cols_here = slot_cols.reshape(-1)
    live_here = live_count.reshape(())
    result = jnp.zeros((slot_total, tile_width, tile_width), jnp.bfloat16)

    def update(slot, current):
        left_tile = lax.dynamic_index_in_dim(
            row_blocks, rows_here[slot] // grid_rows, 0, keepdims=False
        )
        right_tile = lax.dynamic_index_in_dim(
            col_blocks, cols_here[slot] // grid_cols, 0, keepdims=False
        )
        product = lax.dot_general(
            left_tile, right_tile, (((1,), (1,)), ((), ())), preferred_element_type=jnp.float32
        )
        return lax.dynamic_update_index_in_dim(current, (-product).astype(jnp.bfloat16), slot, 0)

    result = lax.fori_loop(0, live_here, update, result)
    return result.reshape(1, 1, slot_total, tile_width, tile_width)


def solution(mesh):
    placed = (
        P(None, "row", "col", None),
        P(),
        P("row", "col", None),
        P("row", "col", None),
        P("row", "col"),
    )
    return jax.shard_map(
        body,
        mesh=mesh,
        in_specs=placed,
        out_specs=P("row", "col", None, None, None),
        check_vma=False,
    )
```

profile of v0, /device:TPU:32, one launch (start us, length us, event | category | flops | bytes accessed | tf_op | source)
XLA Modules:
  0.0 229.6 jit_solution(7024908279362446910)
XLA Ops:
  6.5 0.0 copy-start
  6.5 0.0 all-gather.2.cloned.1.call-start
  6.5 1.0 copy-done
  7.6 1.7 convolution_convert_fusion
  9.3 0.0 all-gather.2.cloned.1.call-update
  9.3 0.0 all-reduce.2.cloned.1.call-start
  9.4 76.0 %all-gather.2.cloned.1.call-done = bf16[4,1,512,512]{3,2,0,1:T(8,128)(2,1)} async-done(((bf16[4,1,16,512]{3,2,0,1:T(8,128)(2,1)}), bf16[4,1,512,512]{3,2,0,1:T(8,128)(2,1)}) %all-gather.2.cloned.1.call-update) | async-done | bytes 2097168 | tf_op jit(solution)/shard_map/all_gather | solution.py:22
  85.3 0.0 copy-start.2
  85.3 0.0 copy-start.3
  85.3 2.3 select_bitcast_fusion
  87.6 0.0 all-reduce.2.cloned.1.call-update
  87.7 115.9 %all-reduce.2.cloned.1.call-done = bf16[2,512,512]{2,1,0:T(8,128)(2,1)} async-done(((bf16[2,512,512]{2,1,0:T(8,128)(2,1)}), bf16[2,512,512]{2,1,0:T(8,128)(2,1)}) %all-reduce.2.cloned.1.call-update) | async-done | bytes 1048592 | tf_op jit(solution)/shard_map/psum | solution.py:9
  203.6 0.1 broadcast_in_dim.15
  203.6 0.0 copy-done.2
  203.6 0.0 copy-done.3
  203.7 18.1 %while.13 = (s32[]{:T(128)}, bf16[2,512,512]{2,1,0:T(8,128)(2,1)S(1)}, s32[]{:T(128)}, s32[2]{0:T(128)S(1)}, bf16[4,512,512]{2,1,0:T(8,128)(2,1)}, /*index=5*/s3...) while((s32[]{:T(128)}, ...), condition=%wide.region_2.3_spmd, body=%wide.region_1.2_spmd.sunk | while | flops 268959776 | bytes 1573451 | solution.py:47
  204.3 0.6 dynamic_slice.51
  207.5 0.6 dynamic_slice.50
  210.7 1.7 fusion.15
  213.1 0.6 dynamic_slice.51
  216.3 0.6 dynamic_slice.50
  219.5 1.7 fusion.15
  221.8 0.0 copy-start.1
  221.8 1.0 copy-done.1
Async XLA Ops:
  6.5 1.0 copy-start
  6.5 78.8 %all-gather.2.cloned.1.call-start = ((), (), s32[]{:S(2)}) async-start(), calls=%async_computation | async-start | bytes 2162688 | tf_op jit(solution)/shard_map/all_gather | solution.py:22
  9.3 194.3 %all-reduce.2.cloned.1.call-start = ((), (), s32[]{:S(2)}) async-start(), calls=%async_computation.1 | async-start | bytes 2097152 | tf_op jit(solution)/shard_map/psum | solution.py:9
  85.3 118.3 %copy-start.2 = (s32[1,1,2]{2,1,0:T(1,128)S(1)}, s32[1,1,2]{2,1,0:T(1,128)}, u32[]{:S(2)}) copy-start(s32[1,1,2]{2,1,0:T(1,128)} %param.9) | copy-start | bytes 28
  85.3 118.3 %copy-start.3 = (s32[1,1,2]{2,1,0:T(1,128)S(1)}, s32[1,1,2]{2,1,0:T(1,128)}, u32[]{:S(2)}) copy-start(s32[1,1,2]{2,1,0:T(1,128)} %param.10) | copy-start | bytes 28
  221.8 1.0 copy-start.1
Sparse Core Ops, SparseCore 0:
  9.5 75.7 all-gather.1
  88.6 114.9 all-reduce.1
where the time goes:
time: 230 us
  waiting for transfers between devices  192 us (83%)
  between operations  13.5 us (6%)
  loops' own time  12.4 us (5%)
  matrix products  5.03 us (2%)
  local copies, waits for them, and re-layouts  4.43 us (2%)
    psum x1, waiting for transfers between devices, broadcast(): return lax.psum(kept, axis)  116 us
    all_gather x1, waiting for transfers between devices, body(): lax.all_gather(solved, 'col', axis=2, tiled=True)  76 us
    another operation x1, loops' own time, body(): result = lax.fori_loop(0, live_here, update, result)  12.4 us
  transfers between devices with their start and end apart: 2, of which 2 were waited for; matrix products, arithmetic and copies ran while one was open for 0% of the time, Pallas kernels for 0%

commit v1 on v0

--- a/solution.py
+++ b/solution.py
@@ -2,6 +2,11 @@
 import jax.numpy as jnp
 from jax import lax
 from jax.sharding import PartitionSpec as P
+
+
+def gather_from_all(array, axis, dim):
+    copies = jnp.concatenate([array] * lax.axis_size(axis), axis=dim)
+    return lax.all_to_all(copies, axis, dim, dim, tiled=True)
 
 
 def broadcast(value, axis, source):
@@ -19,9 +24,7 @@
         panel.reshape(-1, tile_width), inverse_factor, preferred_element_type=jnp.float32
     )
     solved = solved.astype(jnp.bfloat16).reshape(panel_count, 1, part_rows, tile_width)
-    row_blocks = lax.all_gather(solved, "col", axis=2, tiled=True).reshape(
-        panel_count, tile_width, tile_width
-    )
+    row_blocks = gather_from_all(solved, "col", 2).reshape(panel_count, tile_width, tile_width)
     position = lax.axis_index("col")
     grouped = row_blocks.reshape(column_count, col_ratio, tile_width, tile_width)
     picked = lax.dynamic_index_in_dim(grouped, position // grid_rows, 1, keepdims=False)

time: 230 us -> 284 us (1.23)
  local copies, waits for them, and re-layouts: 4.43 us -> 28.1 us
  waiting for transfers between devices: 192 us -> 209 us
  starting transfers between devices: 0.04 us -> 15.4 us
    all_to_all x0 -> x1, waiting for transfers between devices: none -> 100 us  [gather_from_all(): return lax.all_to_all(copies, axis, dim, dim, tiled=True)]
    all_gather x1 -> x0, waiting for transfers between devices: 76 us -> none  [body(): lax.all_gather(solved, 'col', axis=2, tiled=True)]
    unnamed x8 -> x39, local copies, waits for them, and re-layouts: 2.01 us -> 22.8 us
    all_to_all x0 -> x1, starting transfers between devices: none -> 15.4 us  [gather_from_all(): return lax.all_to_all(copies, axis, dim, dim, tiled=True)]
    psum x1, waiting for transfers between devices: 116 us -> 109 us  [broadcast(): return lax.psum(kept, axis)]
  transfers between devices with their start and end apart: 2 -> 2, of which waited for: 2 -> 2; matrix products, arithmetic and copies ran while one was open for 0% -> 1% of each run, Pallas kernels for 0% -> 0%
where the time goes in v1:
time: 284 us
  waiting for transfers between devices  209 us (74%)
  local copies, waits for them, and re-layouts  28.1 us (10%)
  starting transfers between devices  15.4 us (5%)
  between operations  13.5 us (5%)
  loops' own time  12.4 us (4%)
  matrix products  4.39 us (2%)
    psum x1, waiting for transfers between devices, broadcast(): return lax.psum(kept, axis)  109 us
    all_to_all x1, waiting for transfers between devices, gather_from_all(): return lax.all_to_all(copies, axis, dim, dim, tiled=True)  100 us
    unnamed x39, local copies, waits for them, and re-layouts  22.8 us
    all_to_all x1, starting transfers between devices, gather_from_all(): return lax.all_to_all(copies, axis, dim, dim, tiled=True)  15.4 us
    another operation x1, loops' own time, body(): result = lax.fori_loop(0, live_here, update, result)  12.4 us
  transfers between devices with their start and end apart: 2, of which 2 were waited for; matrix products, arithmetic and copies ran while one was open for 1% of the time, Pallas kernels for 0%

profile of v1, /device:TPU:32, one launch (start us, length us, event | category | flops | bytes accessed | tf_op | source)
XLA Modules:
  0.0 283.5 jit_solution(7660368817296090748)
XLA Ops:
  6.5 0.0 copy-start
  6.5 1.0 copy-done
  7.6 1.0 convolution_convert_fusion
  8.6 0.7 constant_dynamic-update-slice_fusion.31
  9.3 0.7 constant_dynamic-update-slice_fusion.30
  10.0 0.7 constant_dynamic-update-slice_fusion.29
  10.6 0.7 constant_dynamic-update-slice_fusion.28
  11.3 0.7 constant_dynamic-update-slice_fusion.27
  12.0 0.7 constant_dynamic-update-slice_fusion.26
  12.7 0.7 constant_dynamic-update-slice_fusion.25
  13.3 0.7 constant_dynamic-update-slice_fusion.24
  14.0 0.7 constant_dynamic-update-slice_fusion.23
  14.7 0.7 constant_dynamic-update-slice_fusion.22
  15.3 0.7 constant_dynamic-update-slice_fusion.21
  16.0 0.7 constant_dynamic-update-slice_fusion.20
  16.7 0.7 constant_dynamic-update-slice_fusion.19
  17.4 0.7 constant_dynamic-update-slice_fusion.18
  18.0 0.7 constant_dynamic-update-slice_fusion.17
  18.7 0.7 constant_dynamic-update-slice_fusion.16
  19.4 0.7 constant_dynamic-update-slice_fusion.15
  20.1 0.7 constant_dynamic-update-slice_fusion.14
  20.7 0.7 constant_dynamic-update-slice_fusion.13
  21.4 0.7 constant_dynamic-update-slice_fusion.12
  22.1 0.7 constant_dynamic-update-slice_fusion.11
  22.7 0.7 constant_dynamic-update-slice_fusion.10
  23.4 0.7 constant_dynamic-update-slice_fusion.9
  24.1 0.7 constant_dynamic-update-slice_fusion.8
  24.7 0.7 constant_dynamic-update-slice_fusion.7
  25.4 0.7 constant_dynamic-update-slice_fusion.6
  26.1 0.7 constant_dynamic-update-slice_fusion.5
  26.8 0.7 constant_dynamic-update-slice_fusion.4
  27.4 0.7 constant_dynamic-update-slice_fusion.3
  28.1 0.7 constant_dynamic-update-slice_fusion.2
  28.8 0.7 constant_dynamic-update-slice_fusion.1
  29.4 0.7 constant_dynamic-update-slice_fusion
  30.1 15.4 %all-to-all-start = ((bf16[4,1,512,512]{3,0,1,2:T(4,128)(2,1)}), bf16[4,1,512,512]{3,0,1,2:T(4,128)(2,1)S(1)}, u32[]{:S(2)}, u32[]{:S(2)}) async-start(bf16[4,1,512,512]{3,0,1,2:T(4,128)(2,1)} %constant_dynamic-update-slice_fusion), calls=%async_computation | async-start | bytes 4194304 | tf_op jit(solution)/shard_map/all_to_all | solution.py:9
  45.5 0.0 all-reduce.2.cloned.1.call-start
  45.6 100.1 %all-to-all-done = bf16[4,1,512,512]{3,0,1,2:T(4,128)(2,1)S(1)} async-done(((bf16[4,1,512,512]{3,0,1,2:T(4,128)(2,1)}), bf16[4,1,512,512]{3,0,1,2:T(4,128)(2,1)S(1)}, u32[]{:S(2)}, u32[]{:S(2)}) %all-to-all-start) | async-done | bytes 2097184 | tf_op jit(solution)/shard_map/all_to_all | solution.py:9
  145.6 0.4 copy.38
  146.0 1.0 select_bitcast_fusion
  147.1 0.0 all-reduce.2.cloned.1.call-update
  147.1 0.0 copy-start.2
  147.1 0.0 copy-start.3
  147.1 1.8 copy.39
  148.9 108.6 %all-reduce.2.cloned.1.call-done = bf16[2,512,512]{2,1,0:T(8,128)(2,1)} async-done(((bf16[2,512,512]{2,1,0:T(8,128)(2,1)}), bf16[2,512,512]{2,1,0:T(8,128)(2,1)}) %all-reduce.2.cloned.1.call-update) | async-done | bytes 1048592 | tf_op jit(solution)/shard_map/psum | solution.py:14
  257.4 0.1 broadcast_in_dim.15
  257.5 0.0 copy-done.2
  257.5 0.0 copy-done.3
  257.5 18.1 %while.13 = (s32[]{:T(128)}, bf16[2,512,512]{2,1,0:T(8,128)(2,1)S(1)}, s32[]{:T(128)}, s32[2]{0:T(128)S(1)}, bf16[4,512,512]{2,1,0:T(8,128)(2,1)}, /*index=5*/s3...) while((s32[]{:T(128)}, ...), condition=%wide.region_2.3_spmd, body=%wide.region_1.2_spmd.sunk | while | flops 268959776 | bytes 1573443 | solution.py:50
  258.2 0.6 dynamic_slice.51
  261.4 0.6 dynamic_slice.50
  264.6 1.7 fusion.15
  266.9 0.6 dynamic_slice.51
  270.1 0.6 dynamic_slice.50
  273.3 1.7 fusion.15
  275.7 0.0 copy-start.1
  275.7 1.0 copy-done.1
Async XLA Ops:
  6.5 1.0 copy-start
  30.1 115.5 %all-to-all-start = ((bf16[4,1,512,512]{3,0,1,2:T(4,128)(2,1)}), bf16[4,1,512,512]{3,0,1,2:T(4,128)(2,1)S(1)}, u32[]{:S(2)}, u32[]{:S(2)}) async-start(bf16[4,1,512,512]{3,0,1,2:T(4,128)(2,1)} %constant_dynamic-update-slice_fusion), calls=%async_computation | async-start | bytes 4194304 | tf_op jit(solution)/shard_map/all_to_all | solution.py:9
  45.5 212.0 %all-reduce.2.cloned.1.call-start = ((), (), s32[]{:S(2)}) async-start(), calls=%async_computation.1 | async-start | bytes 2097152 | tf_op jit(solution)/shard_map/psum | solution.py:14
  147.1 110.4 %copy-start.2 = (s32[1,1,2]{2,1,0:T(1,128)S(1)}, s32[1,1,2]{2,1,0:T(1,128)}, u32[]{:S(2)}) copy-start(s32[1,1,2]{2,1,0:T(1,128)} %param.9) | copy-start | bytes 28
  147.1 110.4 %copy-start.3 = (s32[1,1,2]{2,1,0:T(1,128)S(1)}, s32[1,1,2]{2,1,0:T(1,128)}, u32[]{:S(2)}) copy-start(s32[1,1,2]{2,1,0:T(1,128)} %param.10) | copy-start | bytes 28
  275.7 1.0 copy-start.1
Sparse Core Ops, SparseCore 0:
  147.2 110.1 all-reduce.1
